TPU v7x, 256 devices: a whole 4x4x8 slice. The times are simulated.
256 devices in a mesh: dp: 4 (over x), ep: 64 (over y, z, core).
Axes of the slice: x: 4, y: 4, z: 8, core: 2. Of those that a mesh axis runs over, the one named last changes fastest.
Arguments:
- tokens: bfloat16 [32768, 2048], P(('dp', 'ep'))
- cotangent: bfloat16 [32768, 2048], P(('dp', 'ep'))
- expert_ids: int32 [32768, 8], P(('dp', 'ep')), may hold values from 0 to 63, all different within a row; in each aligned block of 128 rows (0 to 127, 128 to 255, ...) at most 18 rows name the same one
- route_weights: bfloat16 [32768, 8], P(('dp', 'ep')), may hold values from 0.029907227 to 0.3984375
- weights: bfloat16 [64, 3, 2048, 384], P('ep')
- first_moment: bfloat16 [64, 3, 2048, 384], P('ep', None, 'dp'), may hold values from -4 to 4
- second_moment: bfloat16 [64, 3, 2048, 384], P('ep', None, 'dp'), may hold values from 0.049804688 to 0.5
Outputs:
- token_grad: bfloat16 [32768, 2048], P(('dp', 'ep'))
- routing_grad: bfloat16 [32768, 8], P(('dp', 'ep'))
- new_first: bfloat16 [64, 3, 2048, 384], P('ep', None, 'dp')
- new_second: bfloat16 [64, 3, 2048, 384], P('ep', None, 'dp')
- update: bfloat16 [64, 3, 2048, 384], P('ep', None, 'dp')
Inputs may be any that keep to these rules, and one draw needn't show every extreme that they name: `expert_ids`: among the 128 rows of one device no expert is named by more than 18 rows.
All inputs are finite; a program needn't handle non-finite values.
Results may differ from a plain program's by a relative error of at most 0.0057.
Values may be sent and summed in bfloat16 or wider, within the bound.
No kernel may reach another device: no remote copies, remote signals or barrier semaphores. Data moves between devices by JAX's collectives and lax.ppermute only.
A program may use at most 128 MiB of HBM per device.

v0:
```python
import jax
import jax.numpy as jnp
from jax import lax
from jax.experimental.layout import Layout, with_layout_constraint
from jax.sharding import Mesh, PartitionSpec as P

ADAM_STEP = 10
CORES = 2
BF16 = jnp.bfloat16
F32 = jnp.float32
INFO = 128


def plane(mesh):
    dp, ep = mesh.devices.shape
    y = 4
    z = ep // (y * CORES)
    return Mesh(mesh.devices.reshape(dp, y, z, CORES), ("x", "y", "z", "c"))


def on_device(tokens, cotangent, expert_ids, route_weights, weights, first_moment, second_moment):
    tok_count, model_width = tokens.shape
    topk_count = expert_ids.shape[1]
    hidden_units = weights.shape[3]
    ny, nz, nc = (lax.axis_size("y"), lax.axis_size("z"), lax.axis_size("c"))
    experts = ny * nz * nc
    capacity = (tok_count * topk_count * 9 + 8 * experts - 1) // (8 * experts)
    dests = ny * nc
    slots = nz * capacity
    yi, zi, ci = (lax.axis_index("y"), lax.axis_index("z"), lax.axis_index("c"))
    me = ((yi * nz + zi) * nc + ci).astype(F32)
    info = jnp.concatenate([expert_ids.astype(BF16), route_weights], 1)
    info = jnp.pad(info, ((0, 0), (0, INFO - 2 * topk_count)))
    info = with_layout_constraint(info, Layout((0, 1)))
    rows = with_layout_constraint(jnp.concatenate([tokens, info], 1), Layout((0, 1)))
    all_x = lax.all_gather(rows, "z", axis=0, tiled=True)
    all_cot = lax.all_gather(cotangent, "z", axis=0, tiled=True)
    ids = all_x[:, model_width : model_width + topk_count].astype(F32)
    dest = jnp.arange(dests, dtype=jnp.int32)
    dest_expert = ((dest // nc * nz + zi) * nc + dest % nc).astype(F32)
    match = jnp.any(ids[:, :, None] == dest_expert[None, None, :], 1)
    tri = jnp.tril(jnp.ones((tok_count, tok_count), BF16))
    count = jnp.einsum(
        "ab,sbd->sad",
        tri,
        match.astype(BF16).reshape(nz, tok_count, dests),
        preferred_element_type=F32,
    )
    base = (jnp.arange(nz, dtype=jnp.int32) * capacity - 1).astype(F32)[:, None, None]
    slot = jnp.where(match, (count + base).reshape(nz * tok_count, dests), -1.0)
    slot = lax.optimization_barrier(slot.T)
    picks = (
        slot[:, None, :] == jnp.arange(slots, dtype=jnp.int32).astype(F32)[None, :, None]
    ).astype(BF16)
    picks = lax.optimization_barrier(picks.reshape(dests * slots, nz * tok_count))

    def exchange(rows):
        width = rows.shape[1]
        out = lax.all_to_all(
            rows.reshape(dests, slots, width), ("y", "c"), split_axis=0, concat_axis=0, tiled=True
        )
        return out.reshape(dests * slots, width)

    recv = exchange(jnp.dot(picks, all_x, preferred_element_type=F32).astype(BF16))
    recv_cot = exchange(jnp.dot(picks, all_cot, preferred_element_type=F32).astype(BF16))
    recv_x = recv[:, :model_width]
    recv_ids = recv[:, model_width : model_width + topk_count].astype(F32)
    recv_rw = recv[:, model_width + topk_count : model_width + 2 * topk_count].astype(F32)
    mine = recv_ids == me
    row_weight = jnp.sum(jnp.where(mine, recv_rw, 0.0), 1, keepdims=True)
    w_gate, w_up, w_down = (weights[0, 0], weights[0, 1], weights[0, 2])
    gate_val = jnp.dot(recv_x, w_gate, preferred_element_type=F32)
    up_val = jnp.dot(recv_x, w_up, preferred_element_type=F32)
    sigmoid_gate = jax.nn.sigmoid(gate_val)
    activated = gate_val * sigmoid_gate
    hidden = lax.optimization_barrier((activated * up_val).astype(BF16))
    back_val = jnp.dot(recv_cot, w_down, preferred_element_type=F32)
    route_part = jnp.sum(hidden.astype(F32) * back_val, 1, keepdims=True).astype(BF16)
    scaled = row_weight * back_val
    dgate = (scaled * up_val * sigmoid_gate * (1.0 + gate_val * (1.0 - sigmoid_gate))).astype(BF16)
    dup = (scaled * activated).astype(BF16)
    down_cot = (row_weight * recv_cot.astype(F32)).astype(BF16)
    slot_back = jnp.einsum("rh,dh->rd", dgate, w_gate, preferred_element_type=F32)
    slot_back = slot_back + jnp.einsum("rh,dh->rd", dup, w_up, preferred_element_type=F32)
    route_rows = jnp.where(mine, route_part, jnp.zeros((), BF16))
    route_rows = jnp.pad(route_rows, ((0, 0), (0, INFO - topk_count)))
    send_back = jnp.concatenate([slot_back.astype(BF16), route_rows], 1)
    send_back, grad_x, grad_cot = lax.optimization_barrier((send_back, recv_x, down_cot))
    back_rows = exchange(send_back)
    partial = lax.dot_general(
        picks, back_rows, (((0,), (0,)), ((), ())), preferred_element_type=F32
    )
    total = lax.psum_scatter(partial.astype(BF16), "z", scatter_dimension=0, tiled=True)
    token_grad = total[:, :model_width]
    routing_grad = total[:, model_width : model_width + topk_count]
    grad_local = jnp.stack(
        [
            jnp.einsum("rd,rh->dh", grad_x, dgate, preferred_element_type=F32).astype(BF16),
            jnp.einsum("rd,rh->dh", grad_x, dup, preferred_element_type=F32).astype(BF16),
            jnp.einsum("rd,rh->dh", grad_cot, hidden, preferred_element_type=F32).astype(BF16),
        ],
        0,
    )
    grad_share = lax.psum_scatter(grad_local, "x", scatter_dimension=1, tiled=True).astype(F32)[
        None
    ]
    square = jnp.sum(grad_share * grad_share)
    square = jnp.broadcast_to(square, (experts, 1, 128))
    square = lax.all_to_all(square, ("y", "z", "c"), split_axis=0, concat_axis=0, tiled=True)
    square_sum = lax.psum(jnp.sum(square[:, 0, 0]), "x")
    param_count = 3.0 * experts * model_width * hidden_units
    root_mean = jnp.sqrt(square_sum / param_count + 1e-06)
    clip_factor = jnp.minimum(1.0, 0.5 / root_mean)
    clipped = clip_factor * grad_share
    first_next = 0.9 * first_moment.astype(F32) + 0.1 * clipped
    second_next = 0.95 * second_moment.astype(F32) + 0.05 * clipped * clipped
    update = (
        first_next
        / (1.0 - 0.9**ADAM_STEP)
        / (jnp.sqrt(second_next / (1.0 - 0.95**ADAM_STEP)) + 1e-08)
    )
    return (
        token_grad,
        routing_grad,
        first_next.astype(BF16),
        second_next.astype(BF16),
        update.astype(BF16),
    )


def solution(mesh):
    tok = P(("x", "y", "z", "c"), None)
    ep = ("y", "z", "c")
    state = P(ep, None, "x", None)
    return jax.shard_map(
        on_device,
        mesh=plane(mesh),
        in_specs=(tok, tok, tok, tok, P(ep, None, None, None), state, state),
        out_specs=(tok, tok, state, state, state),
        check_vma=False,
    )
```

profile of v0, /device:TPU:1, one launch (start us, length us, event | category | flops | bytes accessed | tf_op | source)
XLA Modules:
  0.0 375.6 jit_solution(4099123066367515721)
XLA Ops:
  8.7 1.9 fusion.34
  11.5 60.1 %all-gather.3.cloned.1.call-done = bf16[1024,2176]{1,0:T(8,128)(2,1)} async-done(((bf16[128,2176]{1,0:T(8,128)(2,1)}), bf16[1024,2176]{1,0:T(8,128)(2,1)}) %all-gather.3.cloned.1.call-update) | async-done | bytes 4456464 | tf_op jit(solution)/shard_map/all_gather | solution.py:36
  71.6 1.0 slice_convert_fusion
  73.5 9.6 %convolution_convert_fusion = bf16[1152,2176]{1,0:T(8,128)(2,1)} fusion(bf16[1152,1024]{1,0:T(8,128)(2,1)S(1)} %fusion.3, bf16[1024,2176]{1,0:T(8,128)(2,1)} %all-gather.3.cloned.1.call-done), kind=kOutput, calls=%fused_computation | convolution fusion | flops 5136334848 | bytes 11829248 | tf_op jit(solution)/shard_map/dot_general | solution.py:64
  83.1 5.3 %all-to-all-start = ((bf16[8,144,2176]{2,1,0:T(8,128)(2,1)}), bf16[8,144,2176]{2,1,0:T(8,128)(2,1)}, u32[]{:S(2)}, u32[]{:S(2)}) async-start(bf16[8,144,2176]{2,1,0:T(8,128)(2,1)} %bitcast.80), calls=%async_computation | async-start | bytes 10027008 | tf_op jit(solution)/shard_map/all_to_all | solution.py:59
  88.5 38.3 %all-gather.5.cloned.1.call-done = bf16[1024,2048]{1,0:T(8,128)(2,1)} async-done(((bf16[128,2048]{1,0:T(8,128)(2,1)}), bf16[1024,2048]{1,0:T(8,128)(2,1)}) %all-gather.5.cloned.1.call-update) | async-done | bytes 4194320 | tf_op jit(solution)/shard_map/all_gather | solution.py:37
  126.8 8.8 %convolution_convert_fusion.1 = bf16[1152,2048]{1,0:T(8,128)(2,1)} fusion(bf16[1152,1024]{1,0:T(8,128)(2,1)S(1)} %fusion.3, bf16[1024,2048]{1,0:T(8,128)(2,1)} %all-gather.5.cloned.1.call-done), kind=kOutput, calls=%fused_computation.6 | convolution fusion | flops 4834197504 | bytes 11272192 | tf_op jit(solution)/shard_map/dot_general | solution.py:65
  135.6 10.4 %all-to-all-done = bf16[8,144,2176]{2,1,0:T(8,128)(2,1)} async-done(((bf16[8,144,2176]{2,1,0:T(8,128)(2,1)}), bf16[8,144,2176]{2,1,0:T(8,128)(2,1)}, u32[]{:S(2)}, u32[]{:S(2)}) %all-to-all-start) | async-done | bytes 5013536 | tf_op jit(solution)/shard_map/all_to_all | solution.py:59
  146.0 5.4 %all-to-all-start.1 = ((bf16[8,144,2048]{2,1,0:T(8,128)(2,1)}), bf16[8,144,2048]{2,1,0:T(8,128)(2,1)}, u32[]{:S(2)}, u32[]{:S(2)}) async-start(bf16[8,144,2048]{2,1,0:T(8,128)(2,1)} %bitcast.82), calls=%async_computation.1 | async-start | bytes 9437184 | tf_op jit(solution)/shard_map/all_to_all | solution.py:59
  151.5 5.3 %slice.43 = bf16[1152,2048]{1,0:T(8,128)(2,1)} slice(bf16[1152,2176]{1,0:T(8,128)(2,1)} %bitcast.7), slice={[0:1152], [0:2048]} | slice | bytes 9437184 | tf_op jit(solution)/shard_map/slice | solution.py:66
  156.8 1.4 select_reduce_fusion
  158.1 6.4 %fusion.19 = f32[1152,384]{0,1:T(8,128)} fusion(bf16[1,3,2048,384]{3,2,1,0:T(8,128)(2,1)} %param.11, bf16[1152,2176]{1,0:T(8,128)(2,1)} %bitcast.7), kind=kOutput, calls=%fused_computation.39 | convolution fusion | flops 1811939328 | bytes 8060928 | tf_op jit(solution)/shard_map/dot_general | solution.py:73
  164.5 6.3 %fusion.16 = f32[1152,384]{0,1:T(8,128)} fusion(bf16[1,3,2048,384]{3,2,1,0:T(8,128)(2,1)} %param.11, bf16[1152,2176]{1,0:T(8,128)(2,1)} %bitcast.7), kind=kOutput, calls=%fused_computation.36 | convolution fusion | flops 1811939328 | bytes 8060928 | tf_op jit(solution)/shard_map/dot_general | solution.py:72
  170.8 35.1 %all-to-all-done.1 = bf16[8,144,2048]{2,1,0:T(8,128)(2,1)} async-done(((bf16[8,144,2048]{2,1,0:T(8,128)(2,1)}), bf16[8,144,2048]{2,1,0:T(8,128)(2,1)}, u32[]{:S(2)}, u32[]{:S(2)}) %all-to-all-start.1) | async-done | bytes 4718624 | tf_op jit(solution)/shard_map/all_to_all | solution.py:59
  205.9 7.9 %multiply_convert_fusion.2 = (bf16[1152,384]{0,1:T(8,128)(2,1)}, bf16[1152,384]{0,1:T(8,128)(2,1)S(1)}, bf16[1152,384]{0,1:T(8,128)(2,1)S(1)}, f32[1152,384]{0,1:T(8,128)S(1)}) fusion(f32[1152]{0:T(1024)S(1)} %select_reduce_fusion, f32[1152,384]{0,1:T(8,128)} %fusion.16, f32[1152,384]{0,1:T(8,128)} %fusion.19, bf16[1152,2048]{1,0:T(8,128)(2,1)} %bitcast.9, ...), kind=kOutput, calls=%fused_computation.30 | convolution fusion | flops 1819017216 | bytes 14258688 | tf_op jit(solution)/shard_map/dot_general | solution.py:77
  214.0 1.2 broadcast_select_fusion
  215.3 2.7 fusion.14
  218.0 4.5 %fusion.1 = bf16[1152,2048]{1,0:T(8,128)(2,1)S(1)} fusion(f32[1152,2048]{1,0:T(8,128)S(1)} %fusion.14, bf16[1152,384]{0,1:T(8,128)(2,1)} %get-tuple-element.41, bf16[1,3,2048,384]{3,2,1,0:T(8,128)(2,1)S(1)} %bitcast.86), kind=kOutput, calls=%fused_computation.5 | convolution fusion | flops 1816657920 | bytes 16613376 | tf_op jit(solution)/shard_map/rh,dh->rd/dot_general | solution.py:84
  222.5 2.7 fusion.2
  225.2 3.2 multiply_convert_fusion
  228.5 2.8 fusion.6
  231.3 2.8 fusion.5
  234.2 2.8 fusion.7
  237.0 2.5 pad_maximum_fusion
  239.6 62.5 %all_to_all.20 = bf16[8,144,2176]{2,1,0:T(8,128)(2,1)S(1)} all-to-all(bf16[8,144,2176]{2,1,0:T(8,128)(2,1)} %bitcast.79), channel_id=1, replica_groups=mesh['x'=4,'y'=4,'z'=8,'c'=2] {'y','c'}, dimensions={0} | all-to-all | bytes 10027008 | tf_op jit(solution)/shard_map/all_to_all | solution.py:59
  302.1 7.9 %convolution_convert_fusion.2 = bf16[1024,2176]{1,0:T(8,128)(2,1)} fusion(bf16[1152,1024]{1,0:T(8,128)(2,1)S(1)} %fusion.3, bf16[1152,2176]{1,0:T(8,128)(2,1)S(1)} %bitcast.81), kind=kOutput, calls=%fused_computation.7 | convolution fusion | flops 5136056320 | bytes 11829248 | tf_op jit(solution)/shard_map/dot_general | solution.py:90
  310.0 2.6 fusion.10
  313.3 15.9 %all_to_all.21 = f32[64,1,128]{2,1,0:T(1,128)S(1)} all-to-all(f32[64,1,128]{2,1,0:T(1,128)S(1)} %broadcast_in_dim.44), channel_id=1, replica_groups=mesh['x'=4,'y'=4,'z'=8,'c'=2] {'y','z','c'}, dimensions={0} | all-to-all | bytes 65536 | tf_op jit(solution)/shard_map/all_to_all | solution.py:109
  329.9 9.8 %psum.7 = f32[]{:T(128)} all-reduce(f32[]{:T(128)} %slice_reduce_fusion), channel_id=1, replica_groups=mesh['x'=4,'y'=4,'z'=8,'c'=2] {'x'}, use_global_device_ids=true, to_apply=%region_7.8 | all-reduce | flops 1 | bytes 8 | tf_op jit(solution)/shard_map/psum | solution.py:110
  340.4 4.8 %divide_convert_fusion = (bf16[1,3,512,384]{3,2,1,0:T(8,128)(2,1)}, bf16[1,3,512,384]{3,2,1,0:T(8,128)(2,1)}, bf16[1,3,512,384]{3,2,1,0:T(8,128)(2,1)}) fusion(bf16[3,512,384]{2,1,0:T(8,128)(2,1)} %reduce-scatter.5.cloned.1.call-done, bf16[1,3,512,384]{3,2,1,0:T(8,128)(2,1)S(1)} %copy-done, bf16[1,3,512,384]{3,2,1,0:T(8,128)(2,1)S(1)} %copy-done.1, f32[]{:T(128)S(6)} %min.3), kind=kLoop, calls=%fused_computation.27 | loop fusion | flops 10616832 | bytes 7077892 | tf_op jit(solution)/shard_map/convert_element_type | solution.py:127
  345.3 20.6 %reduce-scatter.3.cloned.1.call-done = bf16[128,2176]{1,0:T(8,128)(2,1)} async-done(((bf16[1024,2176]{1,0:T(8,128)(2,1)}), bf16[128,2176]{1,0:T(8,128)(2,1)}) %reduce-scatter.3.cloned.1.call-update) | async-done | bytes 557072 | tf_op jit(solution)/shard_map/reduce_scatter | solution.py:93
  367.2 1.9 slice.44
  (46 shorter events, 6.4 us)
Async XLA Ops:
  7.2 64.5 %all-gather.3.cloned.1.call-start = ((), (), s32[]{:S(2)}) async-start(), calls=%async_computation.6 | async-start | bytes 5013504 | tf_op jit(solution)/shard_map/all_gather | solution.py:36
  10.6 116.2 %all-gather.5.cloned.1.call-start = ((), (), s32[]{:S(2)}) async-start(), calls=%async_computation.7 | async-start | bytes 4718592 | tf_op jit(solution)/shard_map/all_gather | solution.py:37
  83.1 62.9 %all-to-all-start = ((bf16[8,144,2176]{2,1,0:T(8,128)(2,1)}), bf16[8,144,2176]{2,1,0:T(8,128)(2,1)}, u32[]{:S(2)}, u32[]{:S(2)}) async-start(bf16[8,144,2176]{2,1,0:T(8,128)(2,1)} %bitcast.80), calls=%async_computation | async-start | bytes 10027008 | tf_op jit(solution)/shard_map/all_to_all | solution.py:59
  146.0 59.9 %all-to-all-start.1 = ((bf16[8,144,2048]{2,1,0:T(8,128)(2,1)}), bf16[8,144,2048]{2,1,0:T(8,128)(2,1)}, u32[]{:S(2)}, u32[]{:S(2)}) async-start(bf16[8,144,2048]{2,1,0:T(8,128)(2,1)} %bitcast.82), calls=%async_computation.1 | async-start | bytes 9437184 | tf_op jit(solution)/shard_map/all_to_all | solution.py:59
  151.5 158.5 %reduce-scatter.5.cloned.1.call-start = ((), (), s32[]{:S(2)}) async-start(), calls=%async_computation.9 | async-start | bytes 5898240 | tf_op jit(solution)/shard_map/reduce_scatter | solution.py:104
  205.9 9.4 %slice-start.2 = ((s8[4718592]{0:T(1024)(128)(4,1)}), s8[4194304]{0:T(1024)(128)(4,1)S(1)}, s32[]{:S(2)}) async-start(s8[4718592]{0:T(1024)(128)(4,1)} %bitcast.85), calls=%async_computation.12 | async-start | bytes 8388608
  205.9 9.4 %slice-start.3 = ((s8[4718592]{0:T(1024)(128)(4,1)}), s8[524288]{0:T(1024)(128)(4,1)S(1)}, s32[]{:S(2)}) async-start(s8[4718592]{0:T(1024)(128)(4,1)} %bitcast.85), calls=%async_computation.13 | async-start | bytes 1048576
  213.8 4.2 %copy-start.2 = (bf16[1152,384]{0,1:T(8,128)(2,1)}, bf16[1152,384]{0,1:T(8,128)(2,1)S(1)}, u32[]{:S(2)}) copy-start(bf16[1152,384]{0,1:T(8,128)(2,1)S(1)} %get-tuple-element.43) | copy-start | bytes 2654212
  218.0 10.5 %slice-start = ((s8[4718592]{0:T(1024)(128)(4,1)}), s8[4194304]{0:T(1024)(128)(4,1)S(1)}, s32[]{:S(2)}) async-start(s8[4718592]{0:T(1024)(128)(4,1)} %bitcast.83), calls=%async_computation.10 | async-start | bytes 8388608
  222.5 6.0 %slice-start.1 = ((s8[4718592]{0:T(1024)(128)(4,1)}), s8[524288]{0:T(1024)(128)(4,1)S(1)}, s32[]{:S(2)}) async-start(s8[4718592]{0:T(1024)(128)(4,1)} %bitcast.83), calls=%async_computation.11 | async-start | bytes 1048576
  225.2 3.3 copy-start.4
  231.3 2.8 copy-start.3
  239.5 126.3 %reduce-scatter.3.cloned.1.call-start = ((), (), s32[]{:S(2)}) async-start(), calls=%async_computation.8 | async-start | bytes 5013504 | tf_op jit(solution)/shard_map/reduce_scatter | solution.py:93
  310.0 30.5 %copy-start = (bf16[1,3,512,384]{3,2,1,0:T(8,128)(2,1)S(1)}, bf16[1,3,512,384]{3,2,1,0:T(8,128)(2,1)}, u32[]{:S(2)}) copy-start(bf16[1,3,512,384]{3,2,1,0:T(8,128)(2,1)} %param.13) | copy-start | bytes 3538948
  310.0 30.5 %copy-start.1 = (bf16[1,3,512,384]{3,2,1,0:T(8,128)(2,1)S(1)}, bf16[1,3,512,384]{3,2,1,0:T(8,128)(2,1)}, u32[]{:S(2)}) copy-start(bf16[1,3,512,384]{3,2,1,0:T(8,128)(2,1)} %param.12) | copy-start | bytes 3538948
Sparse Core Ops, SparseCore 0:
  10.7 60.8 all-gather.2
  73.4 53.3 all-gather.4
  239.6 50.6 reduce-scatter.4
  310.1 55.6 reduce-scatter.2
where the time goes:
time: 376 us
  waiting for transfers between devices  165 us (44%)
  blocking collectives  88.2 us (23%)
  matrix products  62.5 us (17%)
  other arithmetic  24.3 us (6%)
  between operations  14.7 us (4%)
  starting transfers between devices  10.9 us (3%)
  local copies, waits for them, and re-layouts  9.63 us (3%)
    all_to_all x1, blocking collectives, exchange(): lax.all_to_all(rows.reshape(dests, slots, width), ('y', 'c'), split_axis=...  62.5 us
    all_gather x1, waiting for transfers between devices, on_device(): all_x = lax.all_gather(rows, 'z', axis=0, tiled=True)  60.1 us
    all_to_all x2, waiting for transfers between devices, exchange(): lax.all_to_all(rows.reshape(dests, slots, width), ('y', 'c'), split_axis=...  45.6 us
    all_gather x1, waiting for transfers between devices, on_device(): all_cot = lax.all_gather(cotangent, 'z', axis=0, tiled=True)  38.3 us
    reduce_scatter x1, waiting for transfers between devices, on_device(): lax.psum_scatter(partial.astype(BF16), 'z', scatter_dimension=0, tiled=True)  20.6 us
    all_to_all x1, blocking collectives, on_device(): lax.all_to_all(square, ('y', 'z', 'c'), split_axis=0, concat_axis=0, tile...  15.9 us
    all_to_all x2, starting transfers between devices, exchange(): lax.all_to_all(rows.reshape(dests, slots, width), ('y', 'c'), split_axis=...  10.8 us
    psum x1, blocking collectives, on_device(): square_sum = lax.psum(jnp.sum(square[:, 0, 0]), 'x')  9.81 us
  transfers between devices with their start and end apart: 6, of which 5 were waited for; matrix products, arithmetic and copies ran while one was open for 15% of the time, Pallas kernels for 0%

commit v1 on v0

--- a/solution.py
+++ b/solution.py
@@ -33,7 +33,9 @@
     info = jnp.pad(info, ((0, 0), (0, INFO - 2 * topk_count)))
     info = with_layout_constraint(info, Layout((0, 1)))
     rows = with_layout_constraint(jnp.concatenate([tokens, info], 1), Layout((0, 1)))
-    all_x = lax.all_gather(rows, "z", axis=0, tiled=True)
+    all_x = jnp.concatenate(
+        lax.all_to_all(jnp.stack([rows] * lax.axis_size("z")), "z", 0, 0), axis=0
+    )
     all_cot = lax.all_gather(cotangent, "z", axis=0, tiled=True)
     ids = all_x[:, model_width : model_width + topk_count].astype(F32)
     dest = jnp.arange(dests, dtype=jnp.int32)

time: 376 us -> 478 us (1.27); the launches traced: 376 us -> 472 us
  waiting for transfers between devices: 165 us -> 246 us
  local copies, waits for them, and re-layouts: 9.63 us -> 20 us
  starting transfers between devices: 10.9 us -> 20 us
    all_to_all x0 -> x1, waiting for transfers between devices: none -> 141 us  [on_device(): lax.all_to_all(jnp.stack([rows] * lax.axis_size('z')), 'z', 0, 0)]
    all_gather x1 -> x0, waiting for transfers between devices: 60.1 us -> none  [on_device(): all_x = lax.all_gather(rows, 'z', axis=0, tiled=True)]
    all_gather x1, waiting for transfers between devices: 38.3 us -> 0.01 us  [on_device(): all_cot = lax.all_gather(cotangent, 'z', axis=0, tiled=True)]
    all_to_all x2, waiting for transfers between devices: 45.6 us -> 83.4 us  [exchange(): lax.all_to_all(rows.reshape(dests, slots, width), ('y', 'c'), split_axis=...]
    all_to_all x0 -> x1, starting transfers between devices: none -> 9 us  [on_device(): lax.all_to_all(jnp.stack([rows] * lax.axis_size('z')), 'z', 0, 0)]
    all_to_all x0 -> x1, local copies, waits for them, and re-layouts: none -> 6.45 us  [on_device(): lax.all_to_all(jnp.stack([rows] * lax.axis_size('z')), 'z', 0, 0)]
  transfers between devices with their start and end apart: 6 -> 6, of which waited for: 5 -> 4; matrix products, arithmetic and copies ran while one was open for 15% -> 13% of each run, Pallas kernels for 0% -> 0%
where the time goes in v1:
time: 478 us; the launch traced here: 472 us
  waiting for transfers between devices  246 us (51%)
  blocking collectives  86.1 us (18%)
  matrix products  62.5 us (13%)
  other arithmetic  22.5 us (5%)
  local copies, waits for them, and re-layouts  20 us (4%)
  starting transfers between devices  20 us (4%)
  between operations  14.9 us (3%)
    all_to_all x1, waiting for transfers between devices, on_device(): lax.all_to_all(jnp.stack([rows] * lax.axis_size('z')), 'z', 0, 0)  141 us
    all_to_all x2, waiting for transfers between devices, exchange(): lax.all_to_all(rows.reshape(dests, slots, width), ('y', 'c'), split_axis=...  83.4 us
    all_to_all x1, blocking collectives, exchange(): lax.all_to_all(rows.reshape(dests, slots, width), ('y', 'c'), split_axis=...  62.7 us
    reduce_scatter x1, waiting for transfers between devices, on_device(): lax.psum_scatter(partial.astype(BF16), 'z', scatter_dimension=0, tiled=True)  20.5 us
    all_to_all x1, blocking collectives, on_device(): lax.all_to_all(square, ('y', 'z', 'c'), split_axis=0, concat_axis=0, tile...  13.5 us
    all_to_all x2, starting transfers between devices, exchange(): lax.all_to_all(rows.reshape(dests, slots, width), ('y', 'c'), split_axis=...  10.4 us
    psum x1, blocking collectives, on_device(): square_sum = lax.psum(jnp.sum(square[:, 0, 0]), 'x')  9.89 us
    dot_general x1, matrix products, on_device(): jnp.dot(picks, all_x, preferred_element_type=F32).astype(BF16)  9.65 us
  transfers between devices with their start and end apart: 6, of which 4 were waited for; matrix products, arithmetic and copies ran while one was open for 13% of the time, Pallas kernels for 0%

profile of v1, /device:TPU:1, one launch (start us, length us, event | category | flops | bytes accessed | tf_op | source)
XLA Modules:
  0.0 471.6 jit_solution(952504690946329932)
XLA Ops:
  10.1 2.7 stack.10
  12.8 9.0 %all-to-all-start = ((bf16[8,128,2176]{1,2,0:T(8,128)(2,1)}), bf16[8,128,2176]{1,2,0:T(8,128)(2,1)}, u32[]{:S(2)}, u32[]{:S(2)}) async-start(bf16[8,128,2176]{1,2,0:T(8,128)(2,1)} %stack.10), calls=%async_computation | async-start | bytes 8912896 | tf_op jit(solution)/shard_map/all_to_all | solution.py:37
  22.7 140.8 %all-to-all-done = bf16[8,128,2176]{1,2,0:T(8,128)(2,1)} async-done(((bf16[8,128,2176]{1,2,0:T(8,128)(2,1)}), bf16[8,128,2176]{1,2,0:T(8,128)(2,1)}, u32[]{:S(2)}, u32[]{:S(2)}) %all-to-all-start) | async-done | bytes 4456480 | tf_op jit(solution)/shard_map/all_to_all | solution.py:37
  163.5 6.5 %copy.66 = bf16[8,128,2176]{2,1,0:T(8,128)(2,1)} copy(bf16[8,128,2176]{1,2,0:T(8,128)(2,1)} %all-to-all-done) | data formatting | bytes 8912896 | tf_op jit(solution)/shard_map/all_to_all | solution.py:37
  171.7 9.7 %convolution_convert_fusion = bf16[1152,2176]{1,0:T(8,128)(2,1)} fusion(bf16[1152,1024]{1,0:T(8,128)(2,1)S(1)} %fusion.3, bf16[1024,2176]{1,0:T(8,128)(2,1)} %bitcast.84), kind=kOutput, calls=%fused_computation | convolution fusion | flops 5136334848 | bytes 11829248 | tf_op jit(solution)/shard_map/dot_general | solution.py:66
  181.4 5.0 %all-to-all-start.1 = ((bf16[8,144,2176]{2,1,0:T(8,128)(2,1)}), bf16[8,144,2176]{2,1,0:T(8,128)(2,1)}, u32[]{:S(2)}, u32[]{:S(2)}) async-start(bf16[8,144,2176]{2,1,0:T(8,128)(2,1)} %bitcast.81), calls=%async_computation.1 | async-start | bytes 10027008 | tf_op jit(solution)/shard_map/all_to_all | solution.py:61
  186.4 8.8 %convolution_convert_fusion.1 = bf16[1152,2048]{1,0:T(8,128)(2,1)} fusion(bf16[1152,1024]{1,0:T(8,128)(2,1)S(1)} %fusion.3, bf16[1024,2048]{1,0:T(8,128)(2,1)} %all-gather.2.cloned.1.call-done), kind=kOutput, calls=%fused_computation.6 | convolution fusion | flops 4834197504 | bytes 11272192 | tf_op jit(solution)/shard_map/dot_general | solution.py:67
  195.2 48.8 %all-to-all-done.1 = bf16[8,144,2176]{2,1,0:T(8,128)(2,1)} async-done(((bf16[8,144,2176]{2,1,0:T(8,128)(2,1)}), bf16[8,144,2176]{2,1,0:T(8,128)(2,1)}, u32[]{:S(2)}, u32[]{:S(2)}) %all-to-all-start.1) | async-done | bytes 5013536 | tf_op jit(solution)/shard_map/all_to_all | solution.py:61
  244.0 5.4 %all-to-all-start.2 = ((bf16[8,144,2048]{2,1,0:T(8,128)(2,1)}), bf16[8,144,2048]{2,1,0:T(8,128)(2,1)}, u32[]{:S(2)}, u32[]{:S(2)}) async-start(bf16[8,144,2048]{2,1,0:T(8,128)(2,1)} %bitcast.85), calls=%async_computation.2 | async-start | bytes 9437184 | tf_op jit(solution)/shard_map/all_to_all | solution.py:61
  249.9 5.3 %slice.43 = bf16[1152,2048]{1,0:T(8,128)(2,1)} slice(bf16[1152,2176]{1,0:T(8,128)(2,1)} %bitcast.8), slice={[0:1152], [0:2048]} | slice | bytes 9437184 | tf_op jit(solution)/shard_map/slice | solution.py:68
  255.2 1.3 select_reduce_fusion
  256.5 6.3 %fusion.19 = f32[1152,384]{0,1:T(8,128)} fusion(bf16[1,3,2048,384]{3,2,1,0:T(8,128)(2,1)} %param.11, bf16[1152,2176]{1,0:T(8,128)(2,1)} %bitcast.8), kind=kOutput, calls=%fused_computation.39 | convolution fusion | flops 1811939328 | bytes 8060928 | tf_op jit(solution)/shard_map/dot_general | solution.py:75
  262.9 6.3 %fusion.16 = f32[1152,384]{0,1:T(8,128)} fusion(bf16[1,3,2048,384]{3,2,1,0:T(8,128)(2,1)} %param.11, bf16[1152,2176]{1,0:T(8,128)(2,1)} %bitcast.8), kind=kOutput, calls=%fused_computation.36 | convolution fusion | flops 1811939328 | bytes 8060928 | tf_op jit(solution)/shard_map/dot_general | solution.py:74
  269.2 34.7 %all-to-all-done.2 = bf16[8,144,2048]{2,1,0:T(8,128)(2,1)} async-done(((bf16[8,144,2048]{2,1,0:T(8,128)(2,1)}), bf16[8,144,2048]{2,1,0:T(8,128)(2,1)}, u32[]{:S(2)}, u32[]{:S(2)}) %all-to-all-start.2) | async-done | bytes 4718624 | tf_op jit(solution)/shard_map/all_to_all | solution.py:61
  303.8 7.9 %multiply_convert_fusion.2 = (bf16[1152,384]{0,1:T(8,128)(2,1)}, bf16[1152,384]{0,1:T(8,128)(2,1)S(1)}, bf16[1152,384]{0,1:T(8,128)(2,1)S(1)}, f32[1152,384]{0,1:T(8,128)S(1)}) fusion(f32[1152]{0:T(1024)S(1)} %select_reduce_fusion, f32[1152,384]{0,1:T(8,128)} %fusion.16, f32[1152,384]{0,1:T(8,128)} %fusion.19, bf16[1152,2048]{1,0:T(8,128)(2,1)} %bitcast.10, ...), kind=kOutput, calls=%fused_computation.30 | convolution fusion | flops 1819017216 | bytes 14258688 | tf_op jit(solution)/shard_map/dot_general | solution.py:79
  312.0 1.2 broadcast_select_fusion
  313.2 2.7 fusion.14
  315.9 4.4 fusion.1
  320.4 2.7 fusion.2
  323.1 3.2 multiply_convert_fusion
  326.4 2.8 fusion.6
  329.2 2.8 fusion.5
  332.0 2.8 fusion.7
  334.9 2.5 pad_maximum_fusion
  337.4 62.7 %all_to_all.25 = bf16[8,144,2176]{2,1,0:T(8,128)(2,1)S(1)} all-to-all(bf16[8,144,2176]{2,1,0:T(8,128)(2,1)} %bitcast.80), channel_id=1, replica_groups=mesh['x'=4,'y'=4,'z'=8,'c'=2] {'y','c'}, dimensions={0} | all-to-all | bytes 10027008 | tf_op jit(solution)/shard_map/all_to_all | solution.py:61
  400.1 7.9 %convolution_convert_fusion.2 = bf16[1024,2176]{1,0:T(8,128)(2,1)} fusion(bf16[1152,1024]{1,0:T(8,128)(2,1)S(1)} %fusion.3, bf16[1152,2176]{1,0:T(8,128)(2,1)S(1)} %bitcast.82), kind=kOutput, calls=%fused_computation.7 | convolution fusion | flops 5136056320 | bytes 11829248 | tf_op jit(solution)/shard_map/dot_general | solution.py:92
  408.1 2.6 fusion.10
  411.4 13.5 %all_to_all.26 = f32[64,1,128]{2,1,0:T(1,128)S(1)} all-to-all(f32[64,1,128]{2,1,0:T(1,128)S(1)} %broadcast_in_dim.44), channel_id=1, replica_groups=mesh['x'=4,'y'=4,'z'=8,'c'=2] {'y','z','c'}, dimensions={0} | all-to-all | bytes 65536 | tf_op jit(solution)/shard_map/all_to_all | solution.py:111
  425.6 9.9 %psum.7 = f32[]{:T(128)} all-reduce(f32[]{:T(128)} %slice_reduce_fusion), channel_id=1, replica_groups=mesh['x'=4,'y'=4,'z'=8,'c'=2] {'x'}, use_global_device_ids=true, to_apply=%region_7.8 | all-reduce | flops 1 | bytes 8 | tf_op jit(solution)/shard_map/psum | solution.py:112
  436.2 4.8 %divide_convert_fusion = (bf16[1,3,512,384]{3,2,1,0:T(8,128)(2,1)}, bf16[1,3,512,384]{3,2,1,0:T(8,128)(2,1)}, bf16[1,3,512,384]{3,2,1,0:T(8,128)(2,1)}) fusion(bf16[3,512,384]{2,1,0:T(8,128)(2,1)} %reduce-scatter.5.cloned.1.call-done, bf16[1,3,512,384]{3,2,1,0:T(8,128)(2,1)S(1)} %copy-done, bf16[1,3,512,384]{3,2,1,0:T(8,128)(2,1)S(1)} %copy-done.1, f32[]{:T(128)S(6)} %min.3), kind=kLoop, calls=%fused_computation.27 | loop fusion | flops 10616832 | bytes 7077892 | tf_op jit(solution)/shard_map/convert_element_type | solution.py:129
  441.0 20.5 %reduce-scatter.3.cloned.1.call-done = bf16[128,2176]{1,0:T(8,128)(2,1)} async-done(((bf16[1024,2176]{1,0:T(8,128)(2,1)}), bf16[128,2176]{1,0:T(8,128)(2,1)}) %reduce-scatter.3.cloned.1.call-update) | async-done | bytes 557072 | tf_op jit(solution)/shard_map/reduce_scatter | solution.py:95
  463.0 1.9 slice.44
  (49 shorter events, 9.1 us)
Async XLA Ops:
  12.8 150.7 %all-to-all-start = ((bf16[8,128,2176]{1,2,0:T(8,128)(2,1)}), bf16[8,128,2176]{1,2,0:T(8,128)(2,1)}, u32[]{:S(2)}, u32[]{:S(2)}) async-start(bf16[8,128,2176]{1,2,0:T(8,128)(2,1)} %stack.10), calls=%async_computation | async-start | bytes 8912896 | tf_op jit(solution)/shard_map/all_to_all | solution.py:37
  21.8 164.6 %all-gather.2.cloned.1.call-start = ((), (), s32[]{:S(2)}) async-start(), calls=%async_computation.7 | async-start | bytes 4718592 | tf_op jit(solution)/shard_map/all_gather | solution.py:39
  181.4 62.6 %all-to-all-start.1 = ((bf16[8,144,2176]{2,1,0:T(8,128)(2,1)}), bf16[8,144,2176]{2,1,0:T(8,128)(2,1)}, u32[]{:S(2)}, u32[]{:S(2)}) async-start(bf16[8,144,2176]{2,1,0:T(8,128)(2,1)} %bitcast.81), calls=%async_computation.1 | async-start | bytes 10027008 | tf_op jit(solution)/shard_map/all_to_all | solution.py:61
  244.0 59.9 %all-to-all-start.2 = ((bf16[8,144,2048]{2,1,0:T(8,128)(2,1)}), bf16[8,144,2048]{2,1,0:T(8,128)(2,1)}, u32[]{:S(2)}, u32[]{:S(2)}) async-start(bf16[8,144,2048]{2,1,0:T(8,128)(2,1)} %bitcast.85), calls=%async_computation.2 | async-start | bytes 9437184 | tf_op jit(solution)/shard_map/all_to_all | solution.py:61
  249.4 158.7 %reduce-scatter.5.cloned.1.call-start = ((), (), s32[]{:S(2)}) async-start(), calls=%async_computation.9 | async-start | bytes 5898240 | tf_op jit(solution)/shard_map/reduce_scatter | solution.py:106
  303.8 9.4 %slice-start.2 = ((s8[4718592]{0:T(1024)(128)(4,1)}), s8[4194304]{0:T(1024)(128)(4,1)S(1)}, s32[]{:S(2)}) async-start(s8[4718592]{0:T(1024)(128)(4,1)} %bitcast.88), calls=%async_computation.12 | async-start | bytes 8388608
  303.8 9.4 %slice-start.3 = ((s8[4718592]{0:T(1024)(128)(4,1)}), s8[524288]{0:T(1024)(128)(4,1)S(1)}, s32[]{:S(2)}) async-start(s8[4718592]{0:T(1024)(128)(4,1)} %bitcast.88), calls=%async_computation.13 | async-start | bytes 1048576
  311.7 4.2 copy-start.2
  315.9 10.4 %slice-start = ((s8[4718592]{0:T(1024)(128)(4,1)}), s8[4194304]{0:T(1024)(128)(4,1)S(1)}, s32[]{:S(2)}) async-start(s8[4718592]{0:T(1024)(128)(4,1)} %bitcast.86), calls=%async_computation.10 | async-start | bytes 8388608
  320.4 6.0 %slice-start.1 = ((s8[4718592]{0:T(1024)(128)(4,1)}), s8[524288]{0:T(1024)(128)(4,1)S(1)}, s32[]{:S(2)}) async-start(s8[4718592]{0:T(1024)(128)(4,1)} %bitcast.86), calls=%async_computation.11 | async-start | bytes 1048576
  323.1 3.3 copy-start.4
  329.2 2.8 copy-start.3
  337.4 124.2 %reduce-scatter.3.cloned.1.call-start = ((), (), s32[]{:S(2)}) async-start(), calls=%async_computation.8 | async-start | bytes 5013504 | tf_op jit(solution)/shard_map/reduce_scatter | solution.py:95
  408.0 28.2 %copy-start = (bf16[1,3,512,384]{3,2,1,0:T(8,128)(2,1)S(1)}, bf16[1,3,512,384]{3,2,1,0:T(8,128)(2,1)}, u32[]{:S(2)}) copy-start(bf16[1,3,512,384]{3,2,1,0:T(8,128)(2,1)} %param.13) | copy-start | bytes 3538948
  408.0 28.2 %copy-start.1 = (bf16[1,3,512,384]{3,2,1,0:T(8,128)(2,1)S(1)}, bf16[1,3,512,384]{3,2,1,0:T(8,128)(2,1)}, u32[]{:S(2)}) copy-start(bf16[1,3,512,384]{3,2,1,0:T(8,128)(2,1)} %param.12) | copy-start | bytes 3538948
Sparse Core Ops, SparseCore 0:
  24.4 135.5 all-gather.1
  337.5 48.1 reduce-scatter.4
  408.2 53.3 reduce-scatter.2
